TPU v7x, 128 devices: a whole 4x4x4 slice. The times are simulated.
128 devices in a mesh: row: 8 (over y_lo, x), col: 16 (over z, y_hi, core).
Axes of the slice: x: 4, y: 4 (y_hi: 2, y_lo: 2; y = y_hi * 2 + y_lo), z: 4, core: 2. Of those that a mesh axis runs over, the one named last changes fastest.
Arguments:
- sources: bfloat16 [64, 32768], P(None, ('row', 'col')), may hold values from -6 to 6
- near_tiles: bfloat16 [128, 128, 256, 256], P('row', 'col'), may hold values from -0.03125 to 0.03125
- far_left: bfloat16 [128, 128, 32, 256], P('row', 'col'), may hold values from -1 to 1
- far_right: bfloat16 [128, 128, 32, 256], P('row', 'col'), may hold values from -0.03125 to 0.03125
- pattern: int32 [128, 128], P('row', 'col'), may hold values from 0 to 2
- band_end: int32 [128], P('row'), may hold values from 0 to 127, as said below
Outputs:
- image: float32 [64, 32768], P(None, ('row', 'col'))
Inputs may be any that keep to these rules, and one draw needn't show every extreme that they name: band_end[I] is at least I, so the band of every block-row starts at its own cluster; the bands of block-rows 0 to 15 run to the last cluster.
All inputs are finite; a program needn't handle non-finite values.
Results may differ from a plain program's by a relative error of at most 0.0021.
Values may be sent and summed in bfloat16 or wider, within the bound.
A program may use at most 128 MiB of HBM per device.

v0:
```python
import jax
import jax.numpy as jnp
from jax import lax
from jax.sharding import PartitionSpec as P


def shards(sources, near_tiles, far_left, far_right, pattern, band_end):
    row_count = lax.axis_size("row")
    col_count = lax.axis_size("col")
    row_index = lax.axis_index("row")
    col_index = lax.axis_index("col")
    num_cases = sources.shape[0]
    block_size = sources.shape[1]
    row_src = lax.all_gather(sources, "col", axis=1, tiled=True).reshape(
        num_cases, col_count, block_size
    )
    col_src = lax.all_gather(sources, "row", axis=1, tiled=True).reshape(
        num_cases, row_count, block_size
    )
    row_ids = row_index * col_count + jnp.arange(col_count, dtype=jnp.int32)
    col_ids = jnp.arange(row_count, dtype=jnp.int32) * col_count + col_index
    live = (row_ids[:, None] <= col_ids[None, :]) & (col_ids[None, :] <= band_end[:, None])
    near_mask = jnp.where(live & (pattern == 1), 1.0, 0.0).astype(jnp.float32)
    far_mask = jnp.where(live & (pattern == 2), 1.0, 0.0).astype(jnp.float32)
    near_rows = jnp.einsum(
        "ikab,ckb->cika", near_tiles, col_src, preferred_element_type=jnp.float32
    )
    far_coef = jnp.einsum(
        "ikrb,ckb->ikcr", far_right, col_src, preferred_element_type=jnp.float32
    ).astype(jnp.bfloat16)
    far_rows = jnp.einsum("ikra,ikcr->cika", far_left, far_coef, preferred_element_type=jnp.float32)
    row_part = jnp.sum(
        near_rows * near_mask[None, :, :, None] + far_rows * far_mask[None, :, :, None], axis=2
    )
    near_cols = jnp.einsum(
        "ikab,cia->ckib", near_tiles, row_src, preferred_element_type=jnp.float32
    )
    back_coef = jnp.einsum(
        "ikra,cia->ikcr", far_left, row_src, preferred_element_type=jnp.float32
    ).astype(jnp.bfloat16)
    far_cols = jnp.einsum(
        "ikrb,ikcr->ckib", far_right, back_coef, preferred_element_type=jnp.float32
    )
    col_part = jnp.sum(
        near_cols * near_mask.T[None, :, :, None] + far_cols * far_mask.T[None, :, :, None], axis=2
    )
    whole = jnp.zeros((num_cases, row_count, col_count, block_size), jnp.float32)
    whole = lax.dynamic_update_index_in_dim(whole, row_part, row_index, 1)
    column_hit = jnp.arange(col_count, dtype=jnp.int32)[None, None, :, None] == col_index
    whole = whole + jnp.where(column_hit, col_part[:, :, None, :], 0.0)
    result = lax.psum_scatter(
        whole.reshape(num_cases, row_count * col_count * block_size),
        ("row", "col"),
        scatter_dimension=1,
        tiled=True,
    )
    return result


def solution(mesh):
    placed = (
        P(None, ("row", "col")),
        P("row", "col", None, None),
        P("row", "col", None, None),
        P("row", "col", None, None),
        P("row", "col"),
        P("row"),
    )
    return jax.shard_map(
        shards, mesh=mesh, in_specs=placed, out_specs=P(None, ("row", "col")), check_vma=False
    )
```

profile of v0, /device:TPU:0, one launch (start us, length us, event | category | flops | bytes accessed | tf_op | source)
XLA Modules:
  0.0 760.8 jit_solution(4454899091737025960)
XLA Ops:
  6.5 0.0 copy-start
  6.5 0.0 reduce-scatter.2.cloned.1.call-start
  6.6 29.3 %all_gather.7 = bf16[64,2048]{1,0:T(8,128)(2,1)S(1)} all-gather(bf16[64,256]{1,0:T(8,128)(2,1)} %param.6), channel_id=1, replica_groups=mesh['row'=8,'col'=16] {'row'}, dimensions={1}, use_global_device_ids=true | all-gather | bytes 294912 | tf_op jit(solution)/shard_map/all_gather | solution.py:17
  35.8 27.8 %all_gather.6 = bf16[64,4096]{1,0:T(8,128)(2,1)S(1)} all-gather(bf16[64,256]{1,0:T(8,128)(2,1)} %param.6), channel_id=1, replica_groups=mesh['row'=8,'col'=16] {'col'}, dimensions={1}, use_global_device_ids=true | all-gather | bytes 557056 | tf_op jit(solution)/shard_map/all_gather | solution.py:14
  63.7 0.8 and_select_fusion.1
  64.4 0.1 copy.37
  64.5 0.1 copy.33
  64.6 0.1 copy.58
  64.6 0.1 copy.57
  64.7 11.9 %fusion.18 = f32[16,64,8,256]{3,1,2,0:T(8,128)} fusion(bf16[16,8,256,256]{3,2,1,0:T(8,128)(2,1)} %param.7, bf16[64,16,256,1]{2,1,0,3:T(8,128)(2,1)S(1)} %bitcast.59), kind=kOutput, calls=%fused_computation.22 | convolution fusion | flops 1073741824 | bytes 25690112 | tf_op jit(solution)/shard_map/ikab,cia->ckib/dot_general | solution.py:35
  76.6 14.1 %fusion = f32[8,64,16,256]{3,1,2,0:T(8,128)} fusion(bf16[16,8,256,256]{3,2,1,0:T(8,128)(2,1)} %param.7, bf16[64,8,256,1]{2,1,0,3:T(8,128)(2,1)S(1)} %bitcast.64), kind=kOutput, calls=%fused_computation | convolution fusion | flops 1073741824 | bytes 25427968 | tf_op jit(solution)/shard_map/ikab,ckb->cika/dot_general | solution.py:25
  90.7 0.0 copy-start.1
  90.7 0.0 copy-done
  90.7 0.7 fusion.11
  91.4 0.0 slice-start
  91.4 2.4 fusion.10
  93.9 0.0 copy-done.1
  93.9 0.0 slice-start.1
  93.9 4.8 fusion.3
  98.7 1.2 broadcast_select_fusion
  99.8 0.0 slice-done
  99.8 0.0 slice-done.1
  99.8 2.7 fusion.2
  102.5 0.2 fusion.14
  102.8 3.9 copy.59
  106.7 0.0 reduce-scatter.2.cloned.1.call-update
  106.7 647.2 %reduce-scatter.2.cloned.1.call-done = f32[64,256]{1,0:T(8,128)} async-done(((f32[64,32768]{1,0:T(8,128)}), f32[64,256]{1,0:T(8,128)}) %reduce-scatter.2.cloned.1.call-update) | async-done | bytes 65552 | tf_op jit(solution)/shard_map/reduce_scatter | solution.py:51
  (4 shorter events, 0.0 us)
Async XLA Ops:
  6.5 84.2 %copy-start = (bf16[16,8,32,256]{3,2,1,0:T(8,128)(2,1)S(1)}, bf16[16,8,32,256]{3,2,1,0:T(8,128)(2,1)}, u32[]{:S(2)}) copy-start(bf16[16,8,32,256]{3,2,1,0:T(8,128)(2,1)} %param.8) | copy-start | bytes 6291460
  6.5 747.4 %reduce-scatter.2.cloned.1.call-start = ((), (), s32[]{:S(2)}) async-start(), calls=%async_computation.1 | async-start | bytes 8454144 | tf_op jit(solution)/shard_map/reduce_scatter | solution.py:51
  90.7 3.2 copy-start.1
  91.4 8.4 %slice-start = ((s8[8388608]{0:T(1024)(128)(4,1)}), s8[4194304]{0:T(1024)(128)(4,1)S(1)}, s32[]{:S(2)}) async-start(s8[8388608]{0:T(1024)(128)(4,1)} %bitcast.56), calls=%async_computation.2 | async-start | bytes 8388608
  93.9 5.9 slice-start.1
Sparse Core Ops, SparseCore 0:
  106.9 647.0 reduce-scatter.1
where the time goes:
time: 761 us
  waiting for transfers between devices  647 us (85%)
  blocking collectives  57.1 us (8%)
  matrix products  36.5 us (5%)
  between operations  13.5 us (2%)
    reduce_scatter x1, waiting for transfers between devices, shards(): lax.psum_scatter(whole.reshape(num_cases, row_count * col_count * block_s...  647 us
    all_gather x1, blocking collectives, shards(): lax.all_gather(sources, 'row', axis=1, tiled=True)  29.3 us
    all_gather x1, blocking collectives, shards(): lax.all_gather(sources, 'col', axis=1, tiled=True)  27.8 us
  transfers between devices with their start and end apart: 1, of which 1 were waited for; matrix products, arithmetic and copies ran while one was open for 0% of the time, Pallas kernels for 0%

commit v1 on v0

--- a/solution.py
+++ b/solution.py
@@ -2,6 +2,13 @@
 import jax.numpy as jnp
 from jax import lax
 from jax.sharding import PartitionSpec as P
+
+
+def gather_over(x, name, dim):
+    devices = lax.axis_size(name)
+    parts = jnp.stack([x for _ in range(devices)])
+    parts = lax.all_to_all(parts, name, split_axis=0, concat_axis=0)
+    return jnp.concatenate(parts, axis=dim)
 
 
 def shards(sources, near_tiles, far_left, far_right, pattern, band_end):
@@ -14,9 +21,7 @@
     row_src = lax.all_gather(sources, "col", axis=1, tiled=True).reshape(
         num_cases, col_count, block_size
     )
-    col_src = lax.all_gather(sources, "row", axis=1, tiled=True).reshape(
-        num_cases, row_count, block_size
-    )
+    col_src = gather_over(sources, "row", 1).reshape(num_cases, row_count, block_size)
     row_ids = row_index * col_count + jnp.arange(col_count, dtype=jnp.int32)
     col_ids = jnp.arange(row_count, dtype=jnp.int32) * col_count + col_index
     live = (row_ids[:, None] <= col_ids[None, :]) & (col_ids[None, :] <= band_end[:, None])

time: 761 us -> 740 us (0.972)
  blocking collectives: 57.1 us -> 27.8 us
    all_gather x1 -> x0, blocking collectives: 29.3 us -> none  [shards(): lax.all_gather(sources, 'row', axis=1, tiled=True)]
  transfers between devices with their start and end apart: 1 -> 2, of which waited for: 1 -> 1; matrix products, arithmetic and copies ran while one was open for 0% -> 2% of each run, Pallas kernels for 0% -> 0%
where the time goes in v1:
time: 740 us
  waiting for transfers between devices  648 us (88%)
  matrix products  32.8 us (4%)
  blocking collectives  27.8 us (4%)
  between operations  13.5 us (2%)
    reduce_scatter x1, waiting for transfers between devices, shards(): lax.psum_scatter(whole.reshape(num_cases, row_count * col_count * block_s...  648 us
    all_gather x1, blocking collectives, shards(): lax.all_gather(sources, 'col', axis=1, tiled=True)  27.8 us
  transfers between devices with their start and end apart: 2, of which 1 were waited for; matrix products, arithmetic and copies ran while one was open for 2% of the time, Pallas kernels for 0%

profile of v1, /device:TPU:0, one launch (start us, length us, event | category | flops | bytes accessed | tf_op | source)
XLA Modules:
  0.0 740.1 jit_solution(15860736631817048677)
XLA Ops:
  6.5 0.0 copy-start
  6.5 1.7 stack.2
  8.2 5.4 all-to-all-start
  13.6 0.0 reduce-scatter.2.cloned.1.call-start
  13.7 27.8 %all_gather.3 = bf16[64,4096]{1,0:T(8,128)(2,1)S(1)} all-gather(bf16[64,256]{1,0:T(8,128)(2,1)} %param.6), channel_id=1, replica_groups=mesh['row'=8,'col'=16] {'col'}, dimensions={1}, use_global_device_ids=true | all-gather | bytes 557056 | tf_op jit(solution)/shard_map/all_gather | solution.py:21
  41.5 0.8 and_select_fusion.1
  42.3 0.1 copy.34
  42.4 0.1 copy.30
  42.4 0.1 copy.49
  42.5 0.0 copy-done
  42.5 0.7 fusion.11
  43.2 0.0 copy-start.2
  43.3 8.8 %fusion.18 = f32[16,64,8,256]{3,1,2,0:T(8,128)S(1)} fusion(bf16[16,8,256,256]{3,2,1,0:T(8,128)(2,1)} %param.7, bf16[64,16,256,1]{2,1,0,3:T(8,128)(2,1)S(1)} %bitcast.55), kind=kOutput, calls=%fused_computation.22 | convolution fusion | flops 1073741824 | bytes 25690112 | tf_op jit(solution)/shard_map/ikab,cia->ckib/dot_general | solution.py:40
  52.1 0.0 copy-done.2
  52.1 2.2 fusion.3
  54.3 4.3 broadcast_select_fusion
  58.6 0.0 all-to-all-done
  58.6 2.3 fusion.10
  60.9 14.1 %fusion = f32[8,64,16,256]{3,1,2,0:T(8,128)} fusion(bf16[16,8,256,256]{3,2,1,0:T(8,128)(2,1)} %param.7, bf16[8,64,256]{2,1,0:T(8,128)(2,1)S(1)} %all-to-all-done), kind=kOutput, calls=%fused_computation | convolution fusion | flops 1073741824 | bytes 25427968 | tf_op jit(solution)/shard_map/ikab,ckb->cika/dot_general | solution.py:30
  75.0 0.0 copy-start.1
  75.0 4.8 fusion.2
  79.8 1.1 copy-done.1
  80.8 0.2 fusion.14
  81.1 3.9 copy.50
  85.0 0.0 reduce-scatter.2.cloned.1.call-update
  85.0 648.3 %reduce-scatter.2.cloned.1.call-done = f32[64,256]{1,0:T(8,128)} async-done(((f32[64,32768]{1,0:T(8,128)}), f32[64,256]{1,0:T(8,128)}) %reduce-scatter.2.cloned.1.call-update) | async-done | bytes 65552 | tf_op jit(solution)/shard_map/reduce_scatter | solution.py:56
  (3 shorter events, 0.0 us)
Async XLA Ops:
  6.5 36.0 %copy-start = (bf16[16,8,32,256]{3,2,1,0:T(8,128)(2,1)S(1)}, bf16[16,8,32,256]{3,2,1,0:T(8,128)(2,1)}, u32[]{:S(2)}) copy-start(bf16[16,8,32,256]{3,2,1,0:T(8,128)(2,1)} %param.8) | copy-start | bytes 6291460
  8.2 50.4 %all-to-all-start = ((bf16[8,64,256]{2,1,0:T(8,128)(2,1)}), bf16[8,64,256]{2,1,0:T(8,128)(2,1)S(1)}, u32[]{:S(2)}, u32[]{:S(2)}) async-start(bf16[8,64,256]{2,1,0:T(8,128)(2,1)} %stack.2), calls=%async_computation | async-start | bytes 524288 | tf_op jit(solution)/shard_map/all_to_all | solution.py:10
  13.6 719.7 %reduce-scatter.2.cloned.1.call-start = ((), (), s32[]{:S(2)}) async-start(), calls=%async_computation.2 | async-start | bytes 8454144 | tf_op jit(solution)/shard_map/reduce_scatter | solution.py:56
  43.2 8.8 %copy-start.2 = (bf16[16,8,32,256]{3,2,1,0:T(8,128)(2,1)S(1)}, bf16[16,8,32,256]{3,2,1,0:T(8,128)(2,1)}, u32[]{:S(2)}) copy-start(bf16[16,8,32,256]{3,2,1,0:T(8,128)(2,1)} %param.9) | copy-start | bytes 6291460
  75.0 5.8 copy-start.1
Sparse Core Ops, SparseCore 0:
  85.1 648.0 reduce-scatter.1
